TPU v7x, 32 devices: a whole 2x2x4 slice. The times are simulated.
32 devices in a mesh: expert: 8 (over z, y), hidden: 4 (over x, core).
Axes of the slice: x: 2, y: 2, z: 4, core: 2. Of those that a mesh axis runs over, the one named last changes fastest.
Arguments:
- tokens: bfloat16 [2, 6144, 768], P(None, 'expert'), may hold values from -6 to 6
- doc_ids: int32 [2, 8, 768], P(None, 'expert'), may hold values from 0 to 3, never falling along the last dimension, each value on 1 to 384 neighbouring positions
- pad_mask: int32 [2, 6144], P(None, 'expert'), may hold values 0 or 1
- norm1_gain: float32 [768], replicated, may hold values from 0.5 to 1.5
- norm1_bias: float32 [768], replicated, may hold values from -1 to 1
- qkv_weight: bfloat16 [3, 768, 768], P(None, None, 'hidden'), may hold values from -0.3125 to 0.3125
- out_weight: bfloat16 [768, 768], P('hidden'), may hold values from -0.875 to 0.875
- norm2_gain: float32 [768], replicated, may hold values from 0.5 to 1.5
- norm2_bias: float32 [768], replicated, may hold values from -1 to 1
- router: bfloat16 [768, 8], replicated, may hold values from -0.15625 to 0.15625
- routes: int32 [2, 6144, 2], P(None, 'expert'), may hold values from 0 to 7, all different within a row; in each aligned block of 768 rows (0 to 767, 768 to 1535, ..., all dimensions but the last counted through in order) at most 384 rows name the same one
- up_weight: bfloat16 [8, 768, 3072], P('expert', None, 'hidden'), may hold values from -0.21875 to 0.21875
- down_weight: bfloat16 [8, 768, 3072], P('expert', None, 'hidden'), may hold values from -0.15625 to 0.15625
- cotangent: bfloat16 [2, 6144, 768], P(None, 'expert'), may hold values from -6 to 6
Outputs:
- block_out: float32 [2, 6144, 768], P(None, 'expert')
- grad_tokens: float32 [2, 6144, 768], P(None, 'expert')
- grad_norm1_gain: float32 [768], replicated
- grad_norm1_bias: float32 [768], replicated
- grad_qkv: float32 [3, 768, 768], P(None, None, 'hidden')
- grad_out: float32 [768, 768], P('hidden')
- grad_norm2_gain: float32 [768], replicated
- grad_norm2_bias: float32 [768], replicated
- grad_router: float32 [768, 8], replicated
- grad_up: float32 [4, 768, 3072], P(None, 'expert', 'hidden')
- grad_down: float32 [4, 768, 3072], P(None, 'expert', 'hidden')
Inputs may be any that keep to these rules, and one draw needn't show every extreme that they name: `routes`: each token names 2 different experts. In each micro-batch the tokens of one pack name any one expert at most 384 times, a bound that some block reaches. `doc_ids`: within a pack document numbers never fall; each document covers 1 to 384 consecutive tokens, and some covers exactly 384. `pad_mask`: 1 marks a real token, 0 a padding token.
All inputs are finite; a program needn't handle non-finite values. No bound on the sum of `pad_mask` on one device may be relied on, other than what follows from the above.
Results may differ from a plain program's by a relative error of at most 0.028.
Values may be sent and summed in bfloat16 or wider, within the bound.
No kernel may reach another device: no remote copies, remote signals or barrier semaphores. Data moves between devices by JAX's collectives and lax.ppermute only.
A program may use at most 256 MiB of HBM per device.

v0:
```python
import jax
import jax.numpy as jnp
from jax import lax
from jax.sharding import PartitionSpec as P

HEAD_DIM = 64
EPSILON = 1e-05
PRECISE = lax.Precision.HIGHEST
MASKED = -1e30


def layer_norm(values, norm_gain, norm_bias):
    centre = values - jnp.mean(values, -1, keepdims=True)
    spread = jnp.mean(centre * centre, -1, keepdims=True)
    return centre * lax.rsqrt(spread + EPSILON) * norm_gain + norm_bias


def gelu_tanh(values):
    return jax.nn.gelu(values, approximate=True)


def visible(doc_row, pad_row):
    total_rows = doc_row.shape[0]
    query_pos = jnp.arange(total_rows)[:, None]
    key_pos = jnp.arange(total_rows)[None, :]
    same_doc = doc_row[:, None] == doc_row[None, :]
    is_real = (pad_row[None, :] == 1) | (query_pos == key_pos)
    return (key_pos <= query_pos) & same_doc & is_real


def slot_tables(route_rows, experts, capacity):
    flat_routes = route_rows.reshape(-1)
    onehot = (flat_routes[:, None] == jnp.arange(experts, dtype=jnp.int32)[None, :]).astype(
        jnp.int32
    )
    before = jnp.cumsum(onehot, 0) - onehot
    placed = jnp.sum(before * onehot, 1)
    slot_index = flat_routes * capacity + placed
    total_rows = flat_routes.shape[0]
    source = (
        jnp.full((experts * capacity,), total_rows, jnp.int32)
        .at[slot_index]
        .set(jnp.arange(total_rows, dtype=jnp.int32))
    )
    return (slot_index, source)


def masked_scores(queries, key_rows, allowed, score_scale):
    scores = (
        jnp.einsum("qhd,khd->hqk", queries, key_rows, preferred_element_type=jnp.float32)
        * score_scale
    )
    return jnp.where(allowed[None], scores, MASKED)


def attend_forward(queries, key_rows, value_rows, allowed, score_scale):
    scores = masked_scores(queries, key_rows, allowed, score_scale)
    row_peak = jnp.max(scores, -1, keepdims=True)
    exponent = jnp.exp(scores - row_peak)
    row_total = jnp.sum(exponent, -1, keepdims=True)
    attn_weights = (exponent / row_total).astype(jnp.bfloat16)
    output = jnp.einsum(
        "hqk,khd->qhd", attn_weights, value_rows, preferred_element_type=jnp.float32
    )
    return (output, row_peak + jnp.log(row_total))


def attend_backward(queries, key_rows, value_rows, allowed, score_scale, log_total, heads_grad):
    scores = masked_scores(queries, key_rows, allowed, score_scale)
    attn_weights = jnp.exp(scores - log_total)
    weight_grad = jnp.einsum(
        "qhd,khd->hqk", heads_grad, value_rows, preferred_element_type=jnp.float32
    )
    row_delta = jnp.sum(attn_weights * weight_grad, -1, keepdims=True)
    score_grad = (attn_weights * (weight_grad - row_delta)).astype(jnp.bfloat16)
    query_grad = (
        jnp.einsum("hqk,khd->qhd", score_grad, key_rows, preferred_element_type=jnp.float32)
        * score_scale
    )
    key_grad = (
        jnp.einsum("hqk,qhd->khd", score_grad, queries, preferred_element_type=jnp.float32)
        * score_scale
    )
    value_grad = jnp.einsum(
        "hqk,qhd->khd",
        attn_weights.astype(jnp.bfloat16),
        heads_grad,
        preferred_element_type=jnp.float32,
    )
    return (query_grad, key_grad, value_grad)


def shards(
    tokens,
    doc_ids,
    pad_mask,
    norm1_gain,
    norm1_bias,
    qkv_weight,
    out_weight,
    norm2_gain,
    norm2_bias,
    router,
    routes,
    up_weight,
    down_weight,
    cotangent,
):
    micro_count, row_count, feat_width = tokens.shape
    expert_count = router.shape[1]
    top_count = routes.shape[2]
    capacity = 2 * row_count * top_count // expert_count
    local_heads = qkv_weight.shape[2] // HEAD_DIM
    score_scale = HEAD_DIM ** (-0.5)
    trainable = lax.axis_index("expert") >= lax.axis_size("expert") // 2
    up_local = up_weight[0]
    down_local = down_weight[0]
    router_wide = router.astype(jnp.float32)
    zero_row = jnp.zeros((1, feat_width), jnp.bfloat16)
    grad_qkv = jnp.zeros(qkv_weight.shape, jnp.float32)
    grad_proj = jnp.zeros(out_weight.shape, jnp.float32)
    grad_router = jnp.zeros(router.shape, jnp.float32)
    gain1_total = jnp.zeros((feat_width,), jnp.float32)
    bias1_total = jnp.zeros((feat_width,), jnp.float32)
    gain2_total = jnp.zeros((feat_width,), jnp.float32)
    bias2_total = jnp.zeros((feat_width,), jnp.float32)
    expert_acc = (jnp.zeros(up_local.shape, jnp.float32), jnp.zeros(down_local.shape, jnp.float32))
    outputs = []
    input_grads = []
    for micro_idx in range(micro_count):
        inputs = tokens[micro_idx].astype(jnp.float32)
        allowed = visible(doc_ids[micro_idx, 0], pad_mask[micro_idx])
        normed1, norm1_pull = jax.vjp(layer_norm, inputs, norm1_gain, norm1_bias)
        attn_in = normed1.astype(jnp.bfloat16)
        projected = jnp.einsum(
            "rd,cdf->crf", attn_in, qkv_weight, preferred_element_type=jnp.float32
        ).astype(jnp.bfloat16)
        head_view = projected.reshape(3, row_count, local_heads, HEAD_DIM)
        queries, key_rows, value_rows = (head_view[0], head_view[1], head_view[2])
        heads_out, log_total = attend_forward(queries, key_rows, value_rows, allowed, score_scale)
        heads_low = heads_out.reshape(row_count, -1).astype(jnp.bfloat16)
        attn_term = jnp.dot(heads_low, out_weight, preferred_element_type=jnp.float32)
        attention = lax.psum(attn_term.astype(jnp.bfloat16), "hidden").astype(jnp.float32)
        residual = inputs + attention
        normed2, norm2_pull = jax.vjp(layer_norm, residual, norm2_gain, norm2_bias)
        moe_in = normed2.astype(jnp.bfloat16)
        logits = jnp.dot(moe_in, router, preferred_element_type=jnp.float32)
        route_rows = routes[micro_idx]
        picker = (
            route_rows[:, :, None] == jnp.arange(expert_count, dtype=jnp.int32)[None, None, :]
        ).astype(jnp.float32)
        chosen = jnp.sum(picker * logits[:, None, :], -1)
        gate_vals = jax.nn.softmax(chosen, -1)
        slot_index, source = slot_tables(route_rows, expert_count, capacity)
        padded_in = jnp.concatenate([moe_in, zero_row], 0)
        send_rows = padded_in[source // top_count].reshape(expert_count, capacity, feat_width)
        received = lax.all_to_all(
            send_rows, "expert", split_axis=0, concat_axis=0, tiled=True
        ).reshape(-1, feat_width)
        hidden_pre = jnp.dot(received, up_local, preferred_element_type=jnp.float32)
        hidden_act = gelu_tanh(hidden_pre).astype(jnp.bfloat16)
        slice_out = jnp.einsum(
            "rf,df->rd", hidden_act, down_local, preferred_element_type=jnp.float32
        )
        summed = lax.psum(slice_out.astype(jnp.bfloat16), "hidden")
        returned = lax.all_to_all(
            summed.reshape(expert_count, capacity, feat_width),
            "expert",
            split_axis=0,
            concat_axis=0,
            tiled=True,
        )
        flat_back = jnp.concatenate([returned.reshape(-1, feat_width), zero_row], 0)
        expert_rows = flat_back[slot_index].reshape(row_count, top_count, feat_width)
        expert_wide = expert_rows.astype(jnp.float32)
        mixture = jnp.sum(gate_vals[:, :, None] * expert_wide, 1)
        outputs.append(residual + mixture)
        upstream = cotangent[micro_idx].astype(jnp.float32)
        expert_grad = (gate_vals[:, :, None] * upstream[:, None, :]).astype(jnp.bfloat16)
        gate_grad = jnp.sum(upstream[:, None, :] * expert_wide, -1)
        chosen_grad = gate_vals * (gate_grad - jnp.sum(gate_vals * gate_grad, -1, keepdims=True))
        logit_grad = jnp.sum(picker * chosen_grad[:, :, None], 1)
        padded_grad = jnp.concatenate([expert_grad.reshape(-1, feat_width), zero_row], 0)
        send_grad = padded_grad[source].reshape(expert_count, capacity, feat_width)
        grad_rows = lax.all_to_all(
            send_grad, "expert", split_axis=0, concat_axis=0, tiled=True
        ).reshape(-1, feat_width)
        act_grad = jnp.dot(grad_rows, down_local, preferred_element_type=jnp.float32)
        gelu_grad = jax.vjp(gelu_tanh, hidden_pre)[1](act_grad)[0]
        pre_grad = gelu_grad.astype(jnp.bfloat16)
        in_term = jnp.einsum("rf,df->rd", pre_grad, up_local, preferred_element_type=jnp.float32)
        in_summed = lax.psum(in_term.astype(jnp.bfloat16), "hidden")
        in_back = lax.all_to_all(
            in_summed.reshape(expert_count, capacity, feat_width),
            "expert",
            split_axis=0,
            concat_axis=0,
            tiled=True,
        )
        flat_in = jnp.concatenate([in_back.reshape(-1, feat_width), zero_row], 0)
        copies_low = flat_in[slot_index].reshape(row_count, top_count, feat_width)
        copies_grad = copies_low.astype(jnp.float32)
        normed2_grad = jnp.sum(copies_grad, 1) + jnp.dot(
            logit_grad, router_wide.T, precision=PRECISE
        )

        def expert_update(acc_pair):
            return (
                acc_pair[0]
                + jnp.einsum("rd,rf->df", received, pre_grad, preferred_element_type=jnp.float32),
                acc_pair[1]
                + jnp.einsum(
                    "rd,rf->df", grad_rows, hidden_act, preferred_element_type=jnp.float32
                ),
            )

        def expert_keep(acc_pair):
            return acc_pair

        expert_acc = lax.cond(trainable, expert_update, expert_keep, expert_acc)
        grad_router = grad_router + jnp.dot(
            moe_in.astype(jnp.float32).T, logit_grad, precision=PRECISE
        )
        resid_grad, gain2_grad, bias2_grad = norm2_pull(normed2_grad)
        gain2_total = gain2_total + gain2_grad
        bias2_total = bias2_total + bias2_grad
        resid_grad = upstream + resid_grad
        attn_grad = resid_grad.astype(jnp.bfloat16)
        grad_proj = grad_proj + jnp.einsum(
            "rf,rd->fd", heads_low, attn_grad, preferred_element_type=jnp.float32
        )
        heads_grad = jnp.einsum(
            "rd,fd->rf", attn_grad, out_weight, preferred_element_type=jnp.float32
        ).astype(jnp.bfloat16)
        query_grad, key_grad, value_grad = attend_backward(
            queries,
            key_rows,
            value_rows,
            allowed,
            score_scale,
            log_total,
            heads_grad.reshape(row_count, local_heads, HEAD_DIM),
        )
        qkv_grad = (
            jnp.stack([query_grad, key_grad, value_grad])
            .reshape(3, row_count, -1)
            .astype(jnp.bfloat16)
        )
        grad_qkv = grad_qkv + jnp.einsum(
            "rd,crf->cdf", attn_in, qkv_grad, preferred_element_type=jnp.float32
        )
        normed1_term = jnp.einsum(
            "crf,cdf->rd", qkv_grad, qkv_weight, preferred_element_type=jnp.float32
        )
        normed1_grad = lax.psum(normed1_term.astype(jnp.bfloat16), "hidden").astype(jnp.float32)
        input_grad, gain1_grad, bias1_grad = norm1_pull(normed1_grad)
        gain1_total = gain1_total + gain1_grad
        bias1_total = bias1_total + bias1_grad
        input_grads.append(resid_grad + input_grad)
    reduced = (
        lax.psum(gain1_total.astype(jnp.bfloat16), "expert").astype(jnp.float32),
        lax.psum(bias1_total.astype(jnp.bfloat16), "expert").astype(jnp.float32),
        lax.psum(grad_qkv.astype(jnp.bfloat16), "expert").astype(jnp.float32),
        lax.psum(grad_proj.astype(jnp.bfloat16), "expert").astype(jnp.float32),
        lax.psum(gain2_total.astype(jnp.bfloat16), "expert").astype(jnp.float32),
        lax.psum(bias2_total.astype(jnp.bfloat16), "expert").astype(jnp.float32),
        lax.psum(grad_router.astype(jnp.bfloat16), "expert").astype(jnp.float32),
    )
    expert_parts = (
        lax.all_to_all(
            expert_acc[0][None].astype(jnp.bfloat16),
            "expert",
            split_axis=1,
            concat_axis=0,
            tiled=True,
        ).astype(jnp.float32),
        lax.all_to_all(
            expert_acc[1][None].astype(jnp.bfloat16),
            "expert",
            split_axis=1,
            concat_axis=0,
            tiled=True,
        ).astype(jnp.float32),
    )
    half_count = expert_count // 2
    return (
        jnp.stack(outputs),
        jnp.stack(input_grads),
        reduced[0],
        reduced[1],
        reduced[2],
        reduced[3],
        reduced[4],
        reduced[5],
        reduced[6],
        expert_parts[0][half_count:],
        expert_parts[1][half_count:],
    )


def solution(mesh):
    placed = (
        P(None, "expert", None),
        P(None, "expert", None),
        P(None, "expert"),
        P(),
        P(),
        P(None, None, "hidden"),
        P("hidden", None),
        P(),
        P(),
        P(),
        P(None, "expert", None),
        P("expert", None, "hidden"),
        P("expert", None, "hidden"),
        P(None, "expert", None),
    )
    return jax.shard_map(
        shards,
        mesh=mesh,
        in_specs=placed,
        out_specs=(
            P(None, "expert", None),
            P(None, "expert", None),
            P(),
            P(),
            P(None, None, "hidden"),
            P("hidden", None),
            P(),
            P(),
            P(),
            P(None, "expert", "hidden"),
            P(None, "expert", "hidden"),
        ),
        check_vma=False,
    )
```

profile of v0, /device:TPU:0, one launch (start us, length us, event | category | flops | bytes accessed | tf_op | source)
XLA Modules:
  0.0 1665.4 jit_solution(2692091185587568231)
XLA Ops:
  46.8 17.9 %all-reduce.18.cloned.1.call-done = bf16[768,768]{1,0:T(8,128)(2,1)} async-done(((bf16[768,768]{1,0:T(8,128)(2,1)}), bf16[768,768]{1,0:T(8,128)(2,1)}) %all-reduce.18.cloned.1.call-update) | async-done | bytes 1179664 | tf_op jit(solution)/shard_map/psum | solution.py:143
  128.2 14.5 gather_fusion.4
  159.9 14.5 gather_fusion.2
  174.4 78.2 %all-to-all-done.4 = bf16[8,384,768]{2,1,0:T(8,128)(2,1)} async-done(((bf16[8,384,768]{2,1,0:T(8,128)(2,1)}), bf16[8,384,768]{2,1,0:T(8,128)(2,1)}, u32[]{:S(2)}, u32[]{:S(2)}) %all-to-all-start.4) | async-done | bytes 4718624 | tf_op jit(solution)/shard_map/all_to_all | solution.py:185
  257.5 14.5 gather_fusion
  272.1 89.1 %all-to-all-done.2 = bf16[8,384,768]{2,1,0:T(8,128)(2,1)} async-done(((bf16[8,384,768]{2,1,0:T(8,128)(2,1)}), bf16[8,384,768]{2,1,0:T(8,128)(2,1)}, u32[]{:S(2)}, u32[]{:S(2)}) %all-to-all-start.2) | async-done | bytes 4718624 | tf_op jit(solution)/shard_map/all_to_all | solution.py:157
  382.2 14.6 gather_fusion.6
  396.8 72.8 %all-to-all-done = bf16[8,384,768]{2,1,0:T(8,128)(2,1)} async-done(((bf16[8,384,768]{2,1,0:T(8,128)(2,1)}), bf16[8,384,768]{2,1,0:T(8,128)(2,1)}, u32[]{:S(2)}, u32[]{:S(2)}) %all-to-all-start) | async-done | bytes 4718624 | tf_op jit(solution)/shard_map/all_to_all | solution.py:157
  482.1 12.1 fusion.6
  515.4 62.6 %all-to-all-done.6 = bf16[8,384,768]{2,1,0:T(8,128)(2,1)} async-done(((bf16[8,384,768]{2,1,0:T(8,128)(2,1)}), bf16[8,384,768]{2,1,0:T(8,128)(2,1)}, u32[]{:S(2)}, u32[]{:S(2)}) %all-to-all-start.6) | async-done | bytes 4718624 | tf_op jit(solution)/shard_map/all_to_all | solution.py:185
  578.0 11.9 fusion.13
  618.3 32.7 %all-to-all-start.8 = ((bf16[8,2,36864]{2,1,0:T(2,128)(2,1)}), bf16[8,2,36864]{2,1,0:T(2,128)(2,1)}, u32[]{:S(2)}, u32[]{:S(2)}) async-start(bf16[8,2,36864]{2,1,0:T(2,128)(2,1)} %reshape.916), calls=%async_computation.8 | async-start | bytes 2359296 | tf_op jit(solution)/shard_map/all_to_all | solution.py:270
  661.1 18.7 %all-to-all-done.8 = bf16[8,2,36864]{2,1,0:T(2,128)(2,1)} async-done(((bf16[8,2,36864]{2,1,0:T(2,128)(2,1)}), bf16[8,2,36864]{2,1,0:T(2,128)(2,1)}, u32[]{:S(2)}, u32[]{:S(2)}) %all-to-all-start.8) | async-done | bytes 1179680 | tf_op jit(solution)/shard_map/all_to_all | solution.py:270
  679.8 32.5 %all_to_all.58 = bf16[8,2,36864]{2,1,0:T(2,128)(2,1)S(1)} all-to-all(bf16[8,2,36864]{2,1,0:T(2,128)(2,1)S(1)} %reshape.918), channel_id=1, replica_groups=mesh['expert'=8,'hidden'=4] {'expert'}, dimensions={0} | all-to-all | bytes 2359296 | tf_op jit(solution)/shard_map/all_to_all | solution.py:277
  712.3 208.9 %all-reduce.26.cloned.1.call-done = (bf16[8,384,768]{2,1,0:T(8,128)(2,1)}, bf16[8,384,768]{2,1,0:T(8,128)(2,1)}, bf16[8,384,768]{2,1,0:T(8,128)(2,1)}, bf16[8,384,768]{2,1,0:T(8,128)(2,1)}) async-done(((bf16[8,384,768]{2,1,0:T(8,128)(2,1)}, bf16[8,384,768]{2,1,0:T(8,128)(2,1)}, bf16[8,384,768]{2,1,0:T(8,128)(2,1)}, bf16[8,384,768]{2,1,0:T(8,128)(2,1)}), (bf16[8,384,768]{2,1,0:T(8,128)(2,1)}, ...) | async-done | bytes 18874384 | tf_op jit(solution)/shard_map/psum | solution.py:165
  921.3 110.1 %all_to_all.59 = bf16[8,384,768]{2,1,0:T(8,128)(2,1)} all-to-all(bf16[8,384,768]{2,1,0:T(8,128)(2,1)} %get-tuple-element.99), channel_id=1, replica_groups=mesh['expert'=8,'hidden'=4] {'expert'}, dimensions={0} | all-to-all | bytes 9437184 | tf_op jit(solution)/shard_map/all_to_all | solution.py:166
  1031.4 107.6 %all_to_all.60 = bf16[8,384,768]{2,1,0:T(8,128)(2,1)} all-to-all(bf16[8,384,768]{2,1,0:T(8,128)(2,1)S(1)} %copy-done.38), channel_id=1, replica_groups=mesh['expert'=8,'hidden'=4] {'expert'}, dimensions={0} | all-to-all | bytes 9437184 | tf_op jit(solution)/shard_map/all_to_all | solution.py:193
  1139.0 107.5 %all_to_all.61 = bf16[8,384,768]{2,1,0:T(8,128)(2,1)} all-to-all(bf16[8,384,768]{2,1,0:T(8,128)(2,1)S(1)} %bitcast.379), channel_id=1, replica_groups=mesh['expert'=8,'hidden'=4] {'expert'}, dimensions={0} | all-to-all | bytes 9437184 | tf_op jit(solution)/shard_map/all_to_all | solution.py:193
  1296.2 58.5 %all-to-all-done.3 = bf16[8,384,768]{2,1,0:T(8,128)(2,1)} async-done(((bf16[8,384,768]{2,1,0:T(8,128)(2,1)}), bf16[8,384,768]{2,1,0:T(8,128)(2,1)}, u32[]{:S(2)}, u32[]{:S(2)}) %all-to-all-start.3) | async-done | bytes 4718624 | tf_op jit(solution)/shard_map/all_to_all | solution.py:166
  1385.8 13.4 multiply_reduce_fusion.2
  1406.4 13.7 multiply_reduce_fusion.3
  1515.0 47.2 %all-reduce.24.cloned.1.call-done = (bf16[768,768]{1,0:T(8,128)(2,1)}, bf16[768,768]{1,0:T(8,128)(2,1)}) async-done(((bf16[768,768]{1,0:T(8,128)(2,1)}, bf16[768,768]{1,0:T(8,128)(2,1)}), (bf16[768,768]{1,0:T(8,128)(2,1)}, bf16[768,768]{1,0:T(8,128)(2,1)})) %all-reduce.24.cloned.1.call-update) | async-done | bytes 2359312 | tf_op jit(solution)/shard_map/psum | solution.py:255
  1570.1 38.8 %all-reduce.8 = (bf16[768]{0:T(1024)(128)(2,1)}, bf16[768]{0:T(1024)(128)(2,1)}, bf16[768]{0:T(1024)(128)(2,1)}, bf16[768]{0:T(1024)(128)(2,1)}, bf16[768,8]{0,1:T(8,128)(2,1)}) all-reduce(bf16[768]{0:T(1024)(128)(2,1)} %add_convert_fusion.6, ...), channel_id=1, replica_groups=mesh['expert'=8,'hidden'=4] {'expert'}, use_global_device_ids=true, to_apply=%region_56.57 | all-reduce | flops 9216 | bytes 36864 | tf_op jit(solution)/shard_map/psum | solution.py:261
  1617.8 29.0 %all-reduce.22.cloned.1.call-done = (bf16[3,768,192]{1,2,0:T(8,128)(2,1)}, bf16[192,768]{1,0:T(8,128)(2,1)}) async-done(((bf16[3,768,192]{1,2,0:T(8,128)(2,1)}, bf16[192,768]{1,0:T(8,128)(2,1)}), (bf16[3,768,192]{1,2,0:T(8,128)(2,1)}, bf16[192,768]{1,0:T(8,128)(2,1)})) %all-reduce.22.cloned.1.call-update) | async-done | bytes 1179664 | tf_op jit(solution)/shard_map/psum | solution.py:263
  (532 shorter events, 429.3 us)
Async XLA Ops:
  7.2 467.2 %copy-start = (bf16[1,768,768]{2,1,0:T(8,128)(2,1)S(1)}, bf16[1,768,768]{2,1,0:T(8,128)(2,1)}, u32[]{:S(2)}) copy-start(bf16[1,768,768]{2,1,0:T(8,128)(2,1)} %param.29) | copy-start | bytes 3538948
  7.2 57.4 %all-reduce.18.cloned.1.call-start = ((), (), s32[]{:S(2)}) async-start(), calls=%async_computation.10 | async-start | bytes 2359296 | tf_op jit(solution)/shard_map/psum | solution.py:143
  24.2 91.2 %all-reduce.20.cloned.1.call-start = ((), (), s32[]{:S(2)}) async-start(), calls=%async_computation.11 | async-start | bytes 2359296 | tf_op jit(solution)/shard_map/psum | solution.py:143
  26.0 97.0 %copy-start.102 = (s32[768,2]{0,1:T(2,128)}, s32[768,2]{0,1:T(2,128)S(1)}, u32[]{:S(2)}) copy-start(s32[768,2]{0,1:T(2,128)S(1)} %get-tuple-element.125) | copy-start | bytes 18436
  42.6 24.8 %copy-start.89 = (f32[768]{0:T(1024)}, f32[768]{0:T(1024)S(1)}, u32[]{:S(2)}) copy-start(f32[768]{0:T(1024)S(1)} %broadcast_multiply_fusion.3) | copy-start | bytes 9220
  88.1 17.2 %copy-start.138 = (f32[768]{0:T(1024)S(1)}, f32[768]{0:T(1024)}, u32[]{:S(2)}) copy-start(f32[768]{0:T(1024)} %get-tuple-element.75) | copy-start | bytes 9220
  142.7 110.0 %all-to-all-start.4 = ((bf16[8,384,768]{2,1,0:T(8,128)(2,1)}), bf16[8,384,768]{2,1,0:T(8,128)(2,1)}, u32[]{:S(2)}, u32[]{:S(2)}) async-start(bf16[8,384,768]{2,1,0:T(8,128)(2,1)} %bitcast.363), calls=%async_computation.4 | async-start | bytes 9437184 | tf_op jit(solution)/shard_map/all_to_all | solution.py:185
  252.7 108.5 %all-to-all-start.2 = ((bf16[8,384,768]{2,1,0:T(8,128)(2,1)}), bf16[8,384,768]{2,1,0:T(8,128)(2,1)}, u32[]{:S(2)}, u32[]{:S(2)}) async-start(bf16[8,384,768]{2,1,0:T(8,128)(2,1)} %bitcast.366), calls=%async_computation.2 | async-start | bytes 9437184 | tf_op jit(solution)/shard_map/all_to_all | solution.py:157
  361.2 108.5 %all-to-all-start = ((bf16[8,384,768]{2,1,0:T(8,128)(2,1)}), bf16[8,384,768]{2,1,0:T(8,128)(2,1)}, u32[]{:S(2)}, u32[]{:S(2)}) async-start(bf16[8,384,768]{2,1,0:T(8,128)(2,1)} %bitcast.364), calls=%async_computation | async-start | bytes 9437184 | tf_op jit(solution)/shard_map/all_to_all | solution.py:157
  469.6 108.3 %all-to-all-start.6 = ((bf16[8,384,768]{2,1,0:T(8,128)(2,1)}), bf16[8,384,768]{2,1,0:T(8,128)(2,1)}, u32[]{:S(2)}, u32[]{:S(2)}) async-start(bf16[8,384,768]{2,1,0:T(8,128)(2,1)} %bitcast.365), calls=%async_computation.6 | async-start | bytes 9437184 | tf_op jit(solution)/shard_map/all_to_all | solution.py:185
  474.3 447.0 %all-reduce.26.cloned.1.call-start = ((), (), s32[]{:S(2)}) async-start(), calls=%async_computation.14 | async-start | bytes 37748736 | tf_op jit(solution)/shard_map/psum | solution.py:165
  482.0 17.7 %copy-start.152 = (bf16[3072,768]{1,0:T(8,128)(2,1)}, bf16[3072,768]{1,0:T(8,128)(2,1)S(1)}, u32[]{:S(2)}) copy-start(bf16[3072,768]{1,0:T(8,128)(2,1)S(1)} %get-tuple-element.139) | copy-start | bytes 14155780
  617.1 33.9 %copy-start.34 = (f32[768,768]{1,0:T(8,128)S(1)}, f32[768,768]{1,0:T(8,128)}, u32[]{:S(2)}) copy-start(f32[768,768]{1,0:T(8,128)} %copy-done.33) | copy-start | bytes 7077892
  618.3 61.5 %all-to-all-start.8 = ((bf16[8,2,36864]{2,1,0:T(2,128)(2,1)}), bf16[8,2,36864]{2,1,0:T(2,128)(2,1)}, u32[]{:S(2)}, u32[]{:S(2)}) async-start(bf16[8,2,36864]{2,1,0:T(2,128)(2,1)} %reshape.916), calls=%async_computation.8 | async-start | bytes 2359296 | tf_op jit(solution)/shard_map/all_to_all | solution.py:270
  921.3 110.1 %copy-start.38 = (bf16[8,384,768]{2,1,0:T(8,128)(2,1)S(1)}, bf16[8,384,768]{2,1,0:T(8,128)(2,1)}, u32[]{:S(2)}) copy-start(bf16[8,384,768]{2,1,0:T(8,128)(2,1)} %get-tuple-element.100) | copy-start | bytes 14155780
  921.3 217.8 %slice-start.8 = ((s8[4718592]{0:T(1024)(128)(4,1)}), s8[4194304]{0:T(1024)(128)(4,1)S(1)}, s32[]{:S(2)}) async-start(s8[4718592]{0:T(1024)(128)(4,1)} %bitcast.378), calls=%async_computation.23 | async-start | bytes 8388608
  1031.4 107.6 %slice-start.9 = ((s8[4718592]{0:T(1024)(128)(4,1)}), s8[524288]{0:T(1024)(128)(4,1)S(1)}, s32[]{:S(2)}) async-start(s8[4718592]{0:T(1024)(128)(4,1)} %bitcast.378), calls=%async_computation.24 | async-start | bytes 1048576
  1246.5 108.2 %all-to-all-start.3 = ((bf16[8,384,768]{2,1,0:T(8,128)(2,1)}), bf16[8,384,768]{2,1,0:T(8,128)(2,1)}, u32[]{:S(2)}, u32[]{:S(2)}) async-start(bf16[8,384,768]{2,1,0:T(8,128)(2,1)} %get-tuple-element.98), calls=%async_computation.3 | async-start | bytes 9437184 | tf_op jit(solution)/shard_map/all_to_all | solution.py:166
  1251.3 310.9 %all-reduce.24.cloned.1.call-start = ((), (), s32[]{:S(2)}) async-start(), calls=%async_computation.13 | async-start | bytes 4718592 | tf_op jit(solution)/shard_map/psum | solution.py:255
  1406.4 14.9 copy-start.71
  1406.4 14.9 copy-start.84
  1406.4 14.9 copy-start.97
  1406.4 16.3 copy-start.24
  1507.5 139.3 %all-reduce.22.cloned.1.call-start = ((), (), s32[]{:S(2)}) async-start(), calls=%async_computation.12 | async-start | bytes 2359296 | tf_op jit(solution)/shard_map/psum | solution.py:263
  (150 other events, 595.5 us)
Sparse Core Ops, SparseCore 0:
  24.3 40.3 all-reduce.17
  77.7 37.7 all-reduce.19
  601.2 320.0 all-reduce.25
  1507.6 54.4 all-reduce.23
  1566.1 80.6 all-reduce.21
where the time goes:
time: 1680 us; the launch traced here: 1670 us
  waiting for transfers between devices  693 us (41%)
  blocking collectives  397 us (24%)
  local copies, waits for them, and re-layouts  221 us (13%)
  other arithmetic  160 us (10%)
  matrix products  120 us (7%)
  starting transfers between devices  57.9 us (3%)
    all_to_all x2, blocking collectives, shards(): lax.all_to_all(in_summed.reshape(expert_count, capacity, feat_width), 'ex...  215 us
    psum x1, waiting for transfers between devices, shards(): summed = lax.psum(slice_out.astype(jnp.bfloat16), 'hidden')  209 us
    all_to_all x2, waiting for transfers between devices, shards(): lax.all_to_all(send_rows, 'expert', split_axis=0, concat_axis=0, tiled=True)  162 us
    all_to_all x2, waiting for transfers between devices, shards(): lax.all_to_all(send_grad, 'expert', split_axis=0, concat_axis=0, tiled=True)  141 us
    all_to_all x1, blocking collectives, shards(): lax.all_to_all(summed.reshape(expert_count, capacity, feat_width), 'exper...  110 us
    all_to_all x1, waiting for transfers between devices, shards(): lax.all_to_all(summed.reshape(expert_count, capacity, feat_width), 'exper...  58.5 us
    psum x1, waiting for transfers between devices, shards(): lax.psum(normed1_term.astype(jnp.bfloat16), 'hidden').astype(jnp.float32)  47.2 us
    psum x1, blocking collectives, shards(): lax.psum(gain1_total.astype(jnp.bfloat16), 'expert').astype(jnp.float32)  38.8 us
  transfers between devices with their start and end apart: 11, of which 11 were waited for; matrix products, arithmetic and copies ran while one was open for 15% of the time, Pallas kernels for 0%

commit v1 on v0

--- a/solution.py
+++ b/solution.py
@@ -7,6 +7,16 @@
 EPSILON = 1e-05
 PRECISE = lax.Precision.HIGHEST
 MASKED = -1e30
+
+
+def meet_numbers(original, axis_id):
+    big = jnp.concatenate(
+        lax.all_to_all(
+            jnp.stack(jnp.split(original, lax.axis_size(axis_id), axis=1), axis=0), axis_id, 0, 0
+        ),
+        axis=0,
+    )
+    return big
 
 
 def layer_norm(values, norm_gain, norm_bias):
@@ -267,13 +277,7 @@
         lax.psum(grad_router.astype(jnp.bfloat16), "expert").astype(jnp.float32),
     )
     expert_parts = (
-        lax.all_to_all(
-            expert_acc[0][None].astype(jnp.bfloat16),
-            "expert",
-            split_axis=1,
-            concat_axis=0,
-            tiled=True,
-        ).astype(jnp.float32),
+        meet_numbers(expert_acc[0][None].astype(jnp.bfloat16), "expert").astype(jnp.float32),
         lax.all_to_all(
             expert_acc[1][None].astype(jnp.bfloat16),
             "expert",

time: 1680 us -> 1680 us (level)
    psum x2, waiting for transfers between devices: 28 us -> 5.17 us  [shards(): lax.psum(attn_term.astype(jnp.bfloat16), 'hidden').astype(jnp.float32)]
  transfers between devices with their start and end apart: 11 -> 11, of which waited for: 11 -> 10; matrix products, arithmetic and copies ran while one was open for 15% -> 15% of each run, Pallas kernels for 0% -> 0%
where the time goes in v1:
time: 1680 us; the launch traced here: 1670 us
  waiting for transfers between devices  699 us (42%)
  blocking collectives  397 us (24%)
  local copies, waits for them, and re-layouts  225 us (13%)
  other arithmetic  158 us (9%)
  matrix products  120 us (7%)
  starting transfers between devices  56.5 us (3%)
    all_to_all x2, blocking collectives, shards(): lax.all_to_all(in_summed.reshape(expert_count, capacity, feat_width), 'ex...  215 us
    psum x1, waiting for transfers between devices, shards(): summed = lax.psum(slice_out.astype(jnp.bfloat16), 'hidden')  214 us
    all_to_all x2, waiting for transfers between devices, shards(): lax.all_to_all(send_rows, 'expert', split_axis=0, concat_axis=0, tiled=True)  162 us
    all_to_all x2, waiting for transfers between devices, shards(): lax.all_to_all(send_grad, 'expert', split_axis=0, concat_axis=0, tiled=True)  153 us
    all_to_all x1, blocking collectives, shards(): lax.all_to_all(summed.reshape(expert_count, capacity, feat_width), 'exper...  110 us
    all_to_all x1, waiting for transfers between devices, shards(): lax.all_to_all(summed.reshape(expert_count, capacity, feat_width), 'exper...  65.8 us
    psum x1, waiting for transfers between devices, shards(): lax.psum(normed1_term.astype(jnp.bfloat16), 'hidden').astype(jnp.float32)  47.1 us
    psum x1, blocking collectives, shards(): lax.psum(gain1_total.astype(jnp.bfloat16), 'expert').astype(jnp.float32)  38.8 us
  transfers between devices with their start and end apart: 11, of which 10 were waited for; matrix products, arithmetic and copies ran while one was open for 15% of the time, Pallas kernels for 0%

profile of v1, /device:TPU:0, one launch (start us, length us, event | category | flops | bytes accessed | tf_op | source)
XLA Modules:
  0.0 1671.6 jit_solution(18171544478360142291)
XLA Ops:
  134.1 14.5 gather_fusion.4
  154.4 14.5 gather_fusion.2
  168.9 89.7 %all-to-all-done.4 = bf16[8,384,768]{2,1,0:T(8,128)(2,1)} async-done(((bf16[8,384,768]{2,1,0:T(8,128)(2,1)}), bf16[8,384,768]{2,1,0:T(8,128)(2,1)}, u32[]{:S(2)}, u32[]{:S(2)}) %all-to-all-start.4) | async-done | bytes 4718624 | tf_op jit(solution)/shard_map/all_to_all | solution.py:195
  263.5 14.5 gather_fusion
  278.0 89.1 %all-to-all-done.2 = bf16[8,384,768]{2,1,0:T(8,128)(2,1)} async-done(((bf16[8,384,768]{2,1,0:T(8,128)(2,1)}), bf16[8,384,768]{2,1,0:T(8,128)(2,1)}, u32[]{:S(2)}, u32[]{:S(2)}) %all-to-all-start.2) | async-done | bytes 4718624 | tf_op jit(solution)/shard_map/all_to_all | solution.py:167
  388.1 14.6 gather_fusion.6
  402.7 72.9 %all-to-all-done = bf16[8,384,768]{2,1,0:T(8,128)(2,1)} async-done(((bf16[8,384,768]{2,1,0:T(8,128)(2,1)}), bf16[8,384,768]{2,1,0:T(8,128)(2,1)}, u32[]{:S(2)}, u32[]{:S(2)}) %all-to-all-start) | async-done | bytes 4718624 | tf_op jit(solution)/shard_map/all_to_all | solution.py:167
  487.8 12.1 fusion.7
  511.0 10.1 multiply_convert_fusion
  521.1 62.8 %all-to-all-done.6 = bf16[8,384,768]{2,1,0:T(8,128)(2,1)} async-done(((bf16[8,384,768]{2,1,0:T(8,128)(2,1)}), bf16[8,384,768]{2,1,0:T(8,128)(2,1)}, u32[]{:S(2)}, u32[]{:S(2)}) %all-to-all-start.6) | async-done | bytes 4718624 | tf_op jit(solution)/shard_map/all_to_all | solution.py:195
  583.9 12.1 fusion.14
  620.5 31.6 %all-to-all-start.9 = ((bf16[8,2,36864]{2,1,0:T(2,128)(2,1)}), bf16[8,2,36864]{2,1,0:T(2,128)(2,1)S(1)}, u32[]{:S(2)}, u32[]{:S(2)}) async-start(bf16[8,2,36864]{2,1,0:T(2,128)(2,1)} %reshape.921), calls=%async_computation.9 | async-start | bytes 2359296 | tf_op jit(solution)/shard_map/all_to_all | solution.py:281
  657.5 23.4 %all-to-all-done.9 = bf16[8,2,36864]{2,1,0:T(2,128)(2,1)S(1)} async-done(((bf16[8,2,36864]{2,1,0:T(2,128)(2,1)}), bf16[8,2,36864]{2,1,0:T(2,128)(2,1)S(1)}, u32[]{:S(2)}, u32[]{:S(2)}) %all-to-all-start.9) | async-done | bytes 1179680 | tf_op jit(solution)/shard_map/all_to_all | solution.py:281
  680.9 32.7 %all_to_all.54 = bf16[8,1,96,768]{3,2,1,0:T(8,128)(2,1)S(1)} all-to-all(bf16[8,1,96,768]{3,2,1,0:T(8,128)(2,1)} %constant_dynamic-update-slice_fusion), channel_id=1, replica_groups=mesh['expert'=8,'hidden'=4] {'expert'}, dimensions={0} | all-to-all | bytes 2359296 | tf_op jit(solution)/shard_map/all_to_all | solution.py:14
  713.6 213.8 %all-reduce.26.cloned.1.call-done = (bf16[8,384,768]{2,1,0:T(8,128)(2,1)}, bf16[8,384,768]{2,1,0:T(8,128)(2,1)}, bf16[8,384,768]{2,1,0:T(8,128)(2,1)}, bf16[8,384,768]{2,1,0:T(8,128)(2,1)}) async-done(((bf16[8,384,768]{2,1,0:T(8,128)(2,1)}, bf16[8,384,768]{2,1,0:T(8,128)(2,1)}, bf16[8,384,768]{2,1,0:T(8,128)(2,1)}, bf16[8,384,768]{2,1,0:T(8,128)(2,1)}), (bf16[8,384,768]{2,1,0:T(8,128)(2,1)}, ...) | async-done | bytes 18874384 | tf_op jit(solution)/shard_map/psum | solution.py:175
  927.4 110.1 %all_to_all.55 = bf16[8,384,768]{2,1,0:T(8,128)(2,1)} all-to-all(bf16[8,384,768]{2,1,0:T(8,128)(2,1)} %get-tuple-element.206), channel_id=1, replica_groups=mesh['expert'=8,'hidden'=4] {'expert'}, dimensions={0} | all-to-all | bytes 9437184 | tf_op jit(solution)/shard_map/all_to_all | solution.py:176
  1037.6 107.6 %all_to_all.56 = bf16[8,384,768]{2,1,0:T(8,128)(2,1)} all-to-all(bf16[8,384,768]{2,1,0:T(8,128)(2,1)S(1)} %copy-done.39), channel_id=1, replica_groups=mesh['expert'=8,'hidden'=4] {'expert'}, dimensions={0} | all-to-all | bytes 9437184 | tf_op jit(solution)/shard_map/all_to_all | solution.py:203
  1145.2 107.5 %all_to_all.57 = bf16[8,384,768]{2,1,0:T(8,128)(2,1)} all-to-all(bf16[8,384,768]{2,1,0:T(8,128)(2,1)S(1)} %bitcast.411), channel_id=1, replica_groups=mesh['expert'=8,'hidden'=4] {'expert'}, dimensions={0} | all-to-all | bytes 9437184 | tf_op jit(solution)/shard_map/all_to_all | solution.py:203
  1295.2 65.8 %all-to-all-done.3 = bf16[8,384,768]{2,1,0:T(8,128)(2,1)} async-done(((bf16[8,384,768]{2,1,0:T(8,128)(2,1)}), bf16[8,384,768]{2,1,0:T(8,128)(2,1)}, u32[]{:S(2)}, u32[]{:S(2)}) %all-to-all-start.3) | async-done | bytes 4718624 | tf_op jit(solution)/shard_map/all_to_all | solution.py:176
  1391.6 13.8 multiply_reduce_fusion.2
  1412.6 13.7 multiply_reduce_fusion.3
  1521.2 47.1 %all-reduce.24.cloned.1.call-done = (bf16[768,768]{1,0:T(8,128)(2,1)}, bf16[768,768]{1,0:T(8,128)(2,1)}) async-done(((bf16[768,768]{1,0:T(8,128)(2,1)}, bf16[768,768]{1,0:T(8,128)(2,1)}), (bf16[768,768]{1,0:T(8,128)(2,1)}, bf16[768,768]{1,0:T(8,128)(2,1)})) %all-reduce.24.cloned.1.call-update) | async-done | bytes 2359312 | tf_op jit(solution)/shard_map/psum | solution.py:265
  1576.2 38.8 %all-reduce.8 = (bf16[768]{0:T(1024)(128)(2,1)}, bf16[768]{0:T(1024)(128)(2,1)}, bf16[768]{0:T(1024)(128)(2,1)}, bf16[768]{0:T(1024)(128)(2,1)}, bf16[768,8]{0,1:T(8,128)(2,1)}) all-reduce(bf16[768]{0:T(1024)(128)(2,1)} %add_convert_fusion.7, ...), channel_id=1, replica_groups=mesh['expert'=8,'hidden'=4] {'expert'}, use_global_device_ids=true, to_apply=%region_56.57 | all-reduce | flops 9216 | bytes 36864 | tf_op jit(solution)/shard_map/psum | solution.py:271
  1623.9 29.2 %all-reduce.22.cloned.1.call-done = (bf16[3,768,192]{1,2,0:T(8,128)(2,1)}, bf16[192,768]{1,0:T(8,128)(2,1)}) async-done(((bf16[3,768,192]{1,2,0:T(8,128)(2,1)}, bf16[192,768]{1,0:T(8,128)(2,1)}), (bf16[3,768,192]{1,2,0:T(8,128)(2,1)}, bf16[192,768]{1,0:T(8,128)(2,1)})) %all-reduce.22.cloned.1.call-update) | async-done | bytes 1179664 | tf_op jit(solution)/shard_map/psum | solution.py:273
  (561 shorter events, 413.8 us)
Async XLA Ops:
  7.2 473.0 %copy-start = (bf16[1,768,768]{2,1,0:T(8,128)(2,1)S(1)}, bf16[1,768,768]{2,1,0:T(8,128)(2,1)}, u32[]{:S(2)}) copy-start(bf16[1,768,768]{2,1,0:T(8,128)(2,1)} %param.29) | copy-start | bytes 3538948
  7.2 60.7 %all-reduce.18.cloned.1.call-start = ((), (), s32[]{:S(2)}) async-start(), calls=%async_computation.10 | async-start | bytes 2359296 | tf_op jit(solution)/shard_map/psum | solution.py:153
  24.2 97.1 %all-reduce.20.cloned.1.call-start = ((), (), s32[]{:S(2)}) async-start(), calls=%async_computation.11 | async-start | bytes 2359296 | tf_op jit(solution)/shard_map/psum | solution.py:153
  25.6 103.4 %copy-start.119 = (s32[768,2]{0,1:T(2,128)}, s32[768,2]{0,1:T(2,128)S(1)}, u32[]{:S(2)}) copy-start(s32[768,2]{0,1:T(2,128)S(1)} %get-tuple-element.248) | copy-start | bytes 18436
  148.6 110.0 %all-to-all-start.4 = ((bf16[8,384,768]{2,1,0:T(8,128)(2,1)}), bf16[8,384,768]{2,1,0:T(8,128)(2,1)}, u32[]{:S(2)}, u32[]{:S(2)}) async-start(bf16[8,384,768]{2,1,0:T(8,128)(2,1)} %bitcast.400), calls=%async_computation.4 | async-start | bytes 9437184 | tf_op jit(solution)/shard_map/all_to_all | solution.py:195
  258.6 108.5 %all-to-all-start.2 = ((bf16[8,384,768]{2,1,0:T(8,128)(2,1)}), bf16[8,384,768]{2,1,0:T(8,128)(2,1)}, u32[]{:S(2)}, u32[]{:S(2)}) async-start(bf16[8,384,768]{2,1,0:T(8,128)(2,1)} %bitcast.399), calls=%async_computation.2 | async-start | bytes 9437184 | tf_op jit(solution)/shard_map/all_to_all | solution.py:167
  367.1 108.5 %all-to-all-start = ((bf16[8,384,768]{2,1,0:T(8,128)(2,1)}), bf16[8,384,768]{2,1,0:T(8,128)(2,1)}, u32[]{:S(2)}, u32[]{:S(2)}) async-start(bf16[8,384,768]{2,1,0:T(8,128)(2,1)} %bitcast.397), calls=%async_computation | async-start | bytes 9437184 | tf_op jit(solution)/shard_map/all_to_all | solution.py:167
  475.6 108.3 %all-to-all-start.6 = ((bf16[8,384,768]{2,1,0:T(8,128)(2,1)}), bf16[8,384,768]{2,1,0:T(8,128)(2,1)}, u32[]{:S(2)}, u32[]{:S(2)}) async-start(bf16[8,384,768]{2,1,0:T(8,128)(2,1)} %bitcast.398), calls=%async_computation.6 | async-start | bytes 9437184 | tf_op jit(solution)/shard_map/all_to_all | solution.py:195
  480.2 447.3 %all-reduce.26.cloned.1.call-start = ((), (), s32[]{:S(2)}) async-start(), calls=%async_computation.14 | async-start | bytes 37748736 | tf_op jit(solution)/shard_map/psum | solution.py:175
  619.3 32.8 %copy-start.76 = (bf16[1,1,96,768]{3,2,1,0:T(8,128)(2,1)S(1)}, bf16[1,1,96,768]{3,2,1,0:T(8,128)(2,1)}, u32[]{:S(2)}) copy-start(bf16[1,1,96,768]{3,2,1,0:T(8,128)(2,1)} %copy-done.75) | copy-start | bytes 442372
  619.3 33.5 %copy-start.74 = (bf16[1,1,96,768]{3,2,1,0:T(8,128)(2,1)S(1)}, bf16[1,1,96,768]{3,2,1,0:T(8,128)(2,1)}, u32[]{:S(2)}) copy-start(bf16[1,1,96,768]{3,2,1,0:T(8,128)(2,1)} %copy-done.73) | copy-start | bytes 442372
  619.3 34.1 %copy-start.72 = (bf16[1,1,96,768]{3,2,1,0:T(8,128)(2,1)S(1)}, bf16[1,1,96,768]{3,2,1,0:T(8,128)(2,1)}, u32[]{:S(2)}) copy-start(bf16[1,1,96,768]{3,2,1,0:T(8,128)(2,1)} %copy-done.71) | copy-start | bytes 442372
  619.4 34.8 %copy-start.70 = (bf16[1,1,96,768]{3,2,1,0:T(8,128)(2,1)S(1)}, bf16[1,1,96,768]{3,2,1,0:T(8,128)(2,1)}, u32[]{:S(2)}) copy-start(bf16[1,1,96,768]{3,2,1,0:T(8,128)(2,1)} %copy-done.69) | copy-start | bytes 442372
  620.5 34.3 %copy-start.68 = (bf16[1,1,96,768]{3,2,1,0:T(8,128)(2,1)S(1)}, bf16[1,1,96,768]{3,2,1,0:T(8,128)(2,1)}, u32[]{:S(2)}) copy-start(bf16[1,1,96,768]{3,2,1,0:T(8,128)(2,1)} %copy-done.67) | copy-start | bytes 442372
  620.5 35.0 %copy-start.66 = (bf16[1,1,96,768]{3,2,1,0:T(8,128)(2,1)S(1)}, bf16[1,1,96,768]{3,2,1,0:T(8,128)(2,1)}, u32[]{:S(2)}) copy-start(bf16[1,1,96,768]{3,2,1,0:T(8,128)(2,1)} %copy-done.65) | copy-start | bytes 442372
  620.5 35.6 %copy-start.64 = (bf16[1,1,96,768]{3,2,1,0:T(8,128)(2,1)S(1)}, bf16[1,1,96,768]{3,2,1,0:T(8,128)(2,1)}, u32[]{:S(2)}) copy-start(bf16[1,1,96,768]{3,2,1,0:T(8,128)(2,1)} %copy-done.63) | copy-start | bytes 442372
  620.5 36.3 %copy-start.62 = (bf16[1,1,96,768]{3,2,1,0:T(8,128)(2,1)S(1)}, bf16[1,1,96,768]{3,2,1,0:T(8,128)(2,1)}, u32[]{:S(2)}) copy-start(bf16[1,1,96,768]{3,2,1,0:T(8,128)(2,1)} %copy-done.61) | copy-start | bytes 442372
  620.5 60.4 %all-to-all-start.9 = ((bf16[8,2,36864]{2,1,0:T(2,128)(2,1)}), bf16[8,2,36864]{2,1,0:T(2,128)(2,1)S(1)}, u32[]{:S(2)}, u32[]{:S(2)}) async-start(bf16[8,2,36864]{2,1,0:T(2,128)(2,1)} %reshape.921), calls=%async_computation.9 | async-start | bytes 2359296 | tf_op jit(solution)/shard_map/all_to_all | solution.py:281
  927.4 110.1 %copy-start.39 = (bf16[8,384,768]{2,1,0:T(8,128)(2,1)S(1)}, bf16[8,384,768]{2,1,0:T(8,128)(2,1)}, u32[]{:S(2)}) copy-start(bf16[8,384,768]{2,1,0:T(8,128)(2,1)} %get-tuple-element.207) | copy-start | bytes 14155780
  927.4 217.8 %slice-start.8 = ((s8[4718592]{0:T(1024)(128)(4,1)}), s8[4194304]{0:T(1024)(128)(4,1)S(1)}, s32[]{:S(2)}) async-start(s8[4718592]{0:T(1024)(128)(4,1)} %bitcast.410), calls=%async_computation.23 | async-start | bytes 8388608
  1037.6 107.6 %slice-start.9 = ((s8[4718592]{0:T(1024)(128)(4,1)}), s8[524288]{0:T(1024)(128)(4,1)S(1)}, s32[]{:S(2)}) async-start(s8[4718592]{0:T(1024)(128)(4,1)} %bitcast.410), calls=%async_computation.24 | async-start | bytes 1048576
  1252.7 108.3 %all-to-all-start.3 = ((bf16[8,384,768]{2,1,0:T(8,128)(2,1)}), bf16[8,384,768]{2,1,0:T(8,128)(2,1)}, u32[]{:S(2)}, u32[]{:S(2)}) async-start(bf16[8,384,768]{2,1,0:T(8,128)(2,1)} %get-tuple-element.205), calls=%async_computation.3 | async-start | bytes 9437184 | tf_op jit(solution)/shard_map/all_to_all | solution.py:176
  1257.5 310.9 %all-reduce.24.cloned.1.call-start = ((), (), s32[]{:S(2)}) async-start(), calls=%async_computation.13 | async-start | bytes 4718592 | tf_op jit(solution)/shard_map/psum | solution.py:265
  1513.7 139.4 %all-reduce.22.cloned.1.call-start = ((), (), s32[]{:S(2)}) async-start(), calls=%async_computation.12 | async-start | bytes 2359296 | tf_op jit(solution)/shard_map/psum | solution.py:273
  (163 other events, 685.5 us)
Sparse Core Ops, SparseCore 0:
  24.3 40.3 all-reduce.17
  80.9 40.2 all-reduce.19
  607.4 320.0 all-reduce.25
  1513.8 54.4 all-reduce.23
  1572.3 80.7 all-reduce.21
